TPU v7x, 256 devices: a whole 4x4x8 slice. The times are simulated.
256 devices in a mesh: head: 16 (over z, core), tail: 16 (over y, x).
Axes of the slice: x: 4, y: 4, z: 8, core: 2. Of those that a mesh axis runs over, the one named last changes fastest.
Arguments:
- head_emb: bfloat16 [131072, 800], P(('head', 'tail')), may hold values from -48 to 48
- head_state: float32 [131072], P(('head', 'tail')), may hold values from 0.01 to 1
- tail_emb: bfloat16 [64, 128, 800], P('tail'), may hold values from -1.5 to 1.5
- tail_state: float32 [64, 128], P('tail'), may hold values from 0.01 to 1
- relation_emb: bfloat16 [1024, 800], replicated, may hold values from -3.5 to 3.5
- head_rows: int32 [1024, 256], P(('head', 'tail')), may hold values from 0 to 511
- relations: int32 [1024, 256], P(('head', 'tail')), may hold values from 0 to 1023
- tail_offsets: int32 [1024, 256], P(('head', 'tail')), may hold values from 0 to 127
- tail_owner: int32 [1024, 1], P(('head', 'tail')), may hold values from 0 to 15; in each aligned block of 4 rows (0 to 3, 4 to 7, ...) at most 2 rows name the same one
- tail_local: int32 [1024], P(('head', 'tail')), may hold values from 0 to 3
- block_count: int32 [256], P(('head', 'tail')), may hold values from 1 to 4, as said below
- neg_blocks: int32 [8], replicated, may hold values from 0 to 63, as said below
Outputs:
- head_new: bfloat16 [131072, 800], P(('head', 'tail'))
- head_state_new: float32 [131072], P(('head', 'tail'))
- tail_new: bfloat16 [64, 128, 800], P('tail')
- tail_state_new: float32 [64, 128], P('tail')
Inputs may be any that keep to these rules, and one draw needn't show every extreme that they name: `tail_owner`: no tail index owns the tail blocks of more than 2 edge block slots of one device, and in some devices one owns exactly 2. `block_count`: some device has all 4 slots live. `neg_blocks`: distinct tail blocks; the last tail block is always among them.
All inputs are finite; a program needn't handle non-finite values.
Results may differ from a plain program's by a relative error of at most 0.0012.
The roundings to bfloat16 on the way count: a program that leaves them out, or rounds other values in their place, can miss the bound.
Values may be sent and summed in bfloat16 or wider, within the bound.
A program may use at most 128 MiB of HBM per device.

v0:
```python
import math

import jax
import jax.numpy as jnp
from jax import lax
from jax.sharding import PartitionSpec as P

LEARN_RATE = 0.3


def complex_product(left, right):
    half_width = left.shape[-1] // 2
    left_re, left_im = (left[..., :half_width], left[..., half_width:])
    right_re, right_im = (right[..., :half_width], right[..., half_width:])
    return jnp.concatenate(
        [left_re * right_re - left_im * right_im, left_re * right_im + left_im * right_re], axis=-1
    )


def conj_product(left, right):
    half_width = left.shape[-1] // 2
    left_re, left_im = (left[..., :half_width], left[..., half_width:])
    right_re, right_im = (right[..., :half_width], right[..., half_width:])
    return jnp.concatenate(
        [left_re * right_re + left_im * right_im, left_im * right_re - left_re * right_im], axis=-1
    )


def row_adagrad(embedding, adagrad_state, gradient):
    state_next = adagrad_state + jnp.mean(gradient * gradient, axis=-1)
    updated = (
        embedding.astype(jnp.float32) - LEARN_RATE * gradient / jnp.sqrt(state_next)[..., None]
    )
    return (updated.astype(jnp.bfloat16), state_next)


def head_sum(tail_grad):
    return lax.psum(tail_grad, "head")


def per_device(
    head_emb,
    head_state,
    tail_emb,
    tail_state,
    relation_emb,
    head_rows,
    relations,
    tail_offsets,
    tail_owner,
    tail_local,
    block_count,
    neg_blocks,
):
    block_total = tail_local.shape[0]
    edge_count = head_rows.shape[1]
    row_width = head_emb.shape[1]
    span_rows = tail_emb.shape[1]
    owned_blocks = tail_emb.shape[0]
    peer_count = lax.axis_size("tail")
    tail_rank = lax.axis_index("tail")
    capacity = max(2, (2 * block_total + peer_count - 1) // peer_count)
    owner_rank = tail_owner[:, 0]
    positions = jnp.arange(block_total, dtype=jnp.int32)
    same_owner = owner_rank[:, None] == owner_rank[None, :]
    earlier = positions[None, :] < positions[:, None]
    slot_index = jnp.sum((same_owner & earlier).astype(jnp.int32), axis=1)
    slot_place = owner_rank * capacity + slot_index
    global_block = owner_rank * owned_blocks + tail_local
    partition = lax.all_gather(tail_emb, "tail", axis=0, tiled=True)
    chosen = jnp.take(partition, global_block, axis=0)
    mine_ids = neg_blocks - tail_rank * owned_blocks
    is_mine = (mine_ids >= 0) & (mine_ids < owned_blocks)
    own_negs = jnp.where(
        is_mine[:, None, None],
        jnp.take(tail_emb, jnp.clip(mine_ids, 0, owned_blocks - 1), axis=0),
        jnp.zeros((), jnp.bfloat16),
    )
    negatives = lax.psum(own_negs.astype(jnp.float32).astype(jnp.bfloat16), "tail").reshape(
        -1, row_width
    )
    total_edges = block_total * edge_count
    flat_rows = head_rows.reshape(-1)
    block_of = jnp.arange(total_edges, dtype=jnp.int32) // edge_count
    live_mask = (block_of < block_count[0]).astype(jnp.float32)
    tail_index = block_of * span_rows + tail_offsets.reshape(-1)
    tail_vectors = jnp.take(chosen.reshape(-1, row_width), tail_index, axis=0)
    relation_vectors = jnp.take(relation_emb, relations.reshape(-1), axis=0)
    head_vectors = jnp.take(head_emb, flat_rows, axis=0)
    query = complex_product(
        head_vectors.astype(jnp.float32), relation_vectors.astype(jnp.float32)
    ).astype(jnp.bfloat16)
    per_group = math.gcd(block_total, max(1, 512 // edge_count))
    group_rows = per_group * edge_count
    group_count = total_edges // group_rows

    def grouped(values):
        return values.reshape((group_count, group_rows) + values.shape[1:])

    def score_group(neg_total, group_items):
        query_rows, tail_rows, live_rows = group_items
        query_float = query_rows.astype(jnp.float32)
        positive = jnp.sum(query_float * tail_rows.astype(jnp.float32), axis=1)
        negative = lax.dot_general(
            query_rows, negatives, (((1,), (1,)), ((), ())), preferred_element_type=jnp.float32
        )
        largest = jnp.maximum(positive, jnp.max(negative, axis=1))
        pos_exp = jnp.exp(positive - largest)
        neg_exp = jnp.exp(negative - largest[:, None])
        denominator = pos_exp + jnp.sum(neg_exp, axis=1)
        pos_grad = (pos_exp / denominator - 1.0) * live_rows
        neg_grad = (neg_exp / denominator[:, None] * live_rows[:, None]).astype(jnp.bfloat16)
        query_grad = pos_grad[:, None] * tail_rows.astype(jnp.float32) + jnp.dot(
            neg_grad, negatives, preferred_element_type=jnp.float32
        )
        tail_part = pos_grad[:, None] * query_float
        neg_total = neg_total + lax.dot_general(
            neg_grad, query_rows, (((0,), (0,)), ((), ())), preferred_element_type=jnp.float32
        )
        return (neg_total, (query_grad, tail_part))

    neg_start = jnp.zeros((negatives.shape[0], row_width), jnp.float32)
    neg_part, (query_grad, tail_part) = lax.scan(
        score_group, neg_start, (grouped(query), grouped(tail_vectors), grouped(live_mask))
    )
    query_grad = query_grad.reshape(total_edges, row_width)
    tail_part = tail_part.reshape(total_edges, row_width)
    head_grad = (
        jnp.zeros(head_emb.shape, jnp.float32)
        .at[flat_rows]
        .add(conj_product(query_grad, relation_vectors.astype(jnp.float32)))
    )
    block_grad = (
        jnp.zeros((block_total * span_rows, row_width), jnp.float32)
        .at[tail_index]
        .add(tail_part)
        .astype(jnp.bfloat16)
    )
    outgoing = (
        jnp.zeros((peer_count * capacity, span_rows, row_width), jnp.bfloat16)
        .at[slot_place]
        .set(block_grad.reshape(block_total, span_rows, row_width))
    )
    outgoing = outgoing.reshape(peer_count, capacity, span_rows, row_width)
    slot_ids = (
        jnp.zeros((peer_count * capacity,), jnp.int32)
        .at[slot_place]
        .set(tail_local)
        .reshape(peer_count, capacity)
    )
    incoming, incoming_ids = (
        lax.all_to_all(outgoing, "tail", split_axis=0, concat_axis=0, tiled=True),
        lax.all_to_all(slot_ids, "tail", split_axis=0, concat_axis=0, tiled=True),
    )
    which_block = (
        incoming_ids.reshape(-1)[:, None] == jnp.arange(owned_blocks, dtype=jnp.int32)[None, :]
    ).astype(jnp.bfloat16)
    tail_grad = lax.dot_general(
        which_block,
        incoming.reshape(peer_count * capacity, span_rows * row_width),
        (((0,), (0,)), ((), ())),
        preferred_element_type=jnp.float32,
    )
    neg_weights = (
        (mine_ids[:, None] == jnp.arange(owned_blocks, dtype=jnp.int32)[None, :]) & is_mine[:, None]
    ).astype(jnp.float32)
    neg_all = lax.psum(neg_part, ("head", "tail"))
    tail_total = head_sum(tail_grad) + lax.dot_general(
        neg_weights,
        neg_all.reshape(neg_weights.shape[0], span_rows * row_width),
        (((0,), (0,)), ((), ())),
        precision=lax.Precision.HIGHEST,
        preferred_element_type=jnp.float32,
    )
    head_updated, head_state_updated = row_adagrad(head_emb, head_state, head_grad)
    tail_updated, tail_state_updated = row_adagrad(
        tail_emb, tail_state, tail_total.reshape(owned_blocks, span_rows, row_width)
    )
    return (head_updated, head_state_updated, tail_updated, tail_state_updated)


def solution(mesh):
    placed = (
        P(("head", "tail"), None),
        P(("head", "tail")),
        P("tail", None, None),
        P("tail", None),
        P(),
        P(("head", "tail"), None),
        P(("head", "tail"), None),
        P(("head", "tail"), None),
        P(("head", "tail"), None),
        P(("head", "tail")),
        P(("head", "tail")),
        P(),
    )
    return jax.shard_map(
        per_device,
        mesh=mesh,
        in_specs=placed,
        out_specs=(
            P(("head", "tail"), None),
            P(("head", "tail")),
            P("tail", None, None),
            P("tail", None),
        ),
        check_vma=False,
    )
```

profile of v0, /device:TPU:1, one launch (start us, length us, event | category | flops | bytes accessed | tf_op | source)
XLA Modules:
  0.0 729.2 jit_solution(752198037437776522)
XLA Ops:
  10.9 7.6 %all-to-all-start = ((s32[16,1,2]{2,1,0:T(1,128)}), s32[16,1,2]{2,1,0:T(1,128)S(1)}, u32[]{:S(2)}, u32[]{:S(2)}) async-start(s32[16,1,2]{2,1,0:T(1,128)} %bitcast.13), calls=%async_computation | async-start | bytes 16384 | tf_op jit(solution)/shard_map/all_to_all | solution.py:153
  21.5 3.8 copy.82
  26.1 3.1 copy.79
  29.3 5.3 gather_fusion.3
  34.5 5.3 gather_fusion
  48.7 62.8 %all-gather.2.cloned.1.call-done = bf16[64,128,800]{1,2,0:T(8,128)(2,1)} async-done(((bf16[4,128,800]{1,2,0:T(8,128)(2,1)}), bf16[64,128,800]{1,2,0:T(8,128)(2,1)}) %all-gather.2.cloned.1.call-update) | async-done | bytes 13107216 | tf_op jit(solution)/shard_map/all_gather | solution.py:70
  111.5 5.4 gather_fusion.2
  119.6 5.3 gather_fusion.4
  124.9 3.3 broadcast_select_fusion
  128.2 3.5 copy.84
  131.6 81.5 %all-reduce.4.cloned.1.call-done = bf16[1024,800]{1,0:T(8,128)(2,1)} async-done(((bf16[1024,800]{1,0:T(8,128)(2,1)}), bf16[1024,800]{1,0:T(8,128)(2,1)}) %all-reduce.4.cloned.1.call-update) | async-done | bytes 1638416 | tf_op jit(solution)/shard_map/psum | solution.py:79
  213.2 30.7 %while.17 = (s32[]{:T(128)}, f32[1024,800]{0,1:T(8,128)}, f32[2,512,800]{1,2,0:T(8,128)}, f32[2,512,800]{1,2,0:T(8,128)}, bf16[2,512,800]{1,2,0:T(8,128)(2,1)S(1...) while((s32[]{:T(128)}, f32[1024,800]{0,1:T(8,128)}, ...), condition=%wide.region_5.7_spmd.clone, body=%wide.region_1.6_spmd.clone.sunk | while | flops 2527675904 | bytes 74365712 | solution.py:123
  213.2 3.0 fusion.55
  223.6 4.5 select_add_fusion.2
  238.4 5.4 select_add_fusion.2
  243.9 4.4 copy.95
  248.2 10.8 %scatter_custom_fusion.2 = f32[512,800]{1,0:T(8,128)S(1)} fusion(s32[1024]{0:T(1024)S(1)} %bitcast.112, f32[1024,800]{1,0:T(8,128)} %bitcast.92, f32[]{:T(128)} %constant.133.clone.1), kind=kCustom, calls=%fused_computation.49 | custom fusion | flops 819200 | bytes 1638912 | tf_op jit(solution)/shard_map/scatter-add | solution.py:136
  261.7 3.6 broadcast_in_dim.108
  268.1 4.6 all-to-all-start.1
  272.8 4.9 copy.92
  277.6 6.1 reshape.276
  287.4 4.4 copy.85
  291.8 75.6 %all-to-all-done.1 = bf16[16,2,128,800]{2,3,1,0:T(8,128)(2,1)} async-done(((bf16[16,2,128,800]{2,3,1,0:T(8,128)(2,1)}), bf16[16,2,128,800]{2,3,1,0:T(8,128)(2,1)}, u32[]{:S(2)}, u32[]{:S(2)}) %all-to-all-start.1) | async-done | bytes 6553632 | tf_op jit(solution)/shard_map/all_to_all | solution.py:152
  367.4 11.0 %copy.91 = bf16[16,2,128,800]{3,2,1,0:T(8,128)(2,1)} copy(bf16[16,2,128,800]{2,3,1,0:T(8,128)(2,1)} %all-to-all-done.1) | data formatting | bytes 13107200 | tf_op jit(solution)/shard_map/all_to_all | solution.py:152
  378.4 13.6 %reshape.275 = bf16[32,102400]{1,0:T(8,128)(2,1)} reshape(bf16[16,2,128,800]{3,2,1,0:T(8,128)(2,1)} %copy.91) | data formatting | bytes 13107200 | tf_op jit(solution)/shard_map/reshape | solution.py:160
  392.0 5.1 fusion.20
  397.2 6.6 multiply_add_fusion
  403.8 10.9 %scatter_custom_fusion = f32[512,800]{1,0:T(8,128)S(1)} fusion(s32[1024]{0:T(1024)S(1)} %bitcast.113, f32[1024,400]{1,0:T(8,128)} %get-tuple-element.225, f32[]{:T(128)} %constant.164, f32[1024,400]{1,0:T(8,128)} %get-tuple-element.224, f32[]{:T(128)} %constant.133.clone.1), kind=kCustom, calls=%fused_computation.32 | custom fusion | flops 1638400 | bytes 4915208 | tf_op jit(solution)/shard_map/scatter-add | solution.py:131
  419.0 171.7 %all-reduce.8.cloned.1.call-done = f32[8,102400]{1,0:T(8,128)} async-done(((f32[8,102400]{1,0:T(8,128)}), f32[8,102400]{1,0:T(8,128)}) %all-reduce.8.cloned.1.call-update) | async-done | bytes 3276816 | tf_op jit(solution)/shard_map/psum | solution.py:167
  590.7 116.5 %all-reduce.6.cloned.1.call-done = f32[4,102400]{1,0:T(4,128)} async-done(((f32[4,102400]{1,0:T(4,128)}), f32[4,102400]{1,0:T(4,128)}) %all-reduce.6.cloned.1.call-update) | async-done | bytes 1638416 | tf_op jit(solution)/shard_map/psum | solution.py:38
  707.2 5.1 broadcast_multiply_fusion
  715.5 3.1 mul.157
  (125 shorter events, 56.5 us)
Async XLA Ops:
  7.2 12.1 %copy-start.3 = (bf16[4,128,800]{1,2,0:T(8,128)(2,1)S(1)}, bf16[4,128,800]{1,2,0:T(8,128)(2,1)}, u32[]{:S(2)}) copy-start(bf16[4,128,800]{1,2,0:T(8,128)(2,1)} %param.18) | copy-start | bytes 2457604
  7.2 104.3 %all-gather.2.cloned.1.call-start = ((), (), s32[]{:S(2)}) async-start(), calls=%async_computation.3 | async-start | bytes 13926400 | tf_op jit(solution)/shard_map/all_gather | solution.py:70
  10.9 257.2 %all-to-all-start = ((s32[16,1,2]{2,1,0:T(1,128)}), s32[16,1,2]{2,1,0:T(1,128)S(1)}, u32[]{:S(2)}, u32[]{:S(2)}) async-start(s32[16,1,2]{2,1,0:T(1,128)} %bitcast.13), calls=%async_computation | async-start | bytes 16384 | tf_op jit(solution)/shard_map/all_to_all | solution.py:153
  18.5 194.7 %all-reduce.4.cloned.1.call-start = ((), (), s32[]{:S(2)}) async-start(), calls=%async_computation.2 | async-start | bytes 3670016 | tf_op jit(solution)/shard_map/psum | solution.py:79
  21.5 3.8 copy-start.12
  21.5 3.9 copy-start.15
  21.5 3.9 copy-start.16
  21.5 3.9 copy-start.9
  26.1 3.1 copy-start.10
  42.4 1.8 copy-start.1
  44.2 3.1 copy-start.11
  45.4 1.9 copy-start.6
  213.2 3.1 copy-start.2
  213.2 3.9 copy-start.17
  216.2 4.1 copy-start
  216.2 2.7 copy-start.7
  220.3 1.8 copy-start.8
  228.1 3.1 copy-start.2
  228.1 3.9 copy-start.17
  231.1 4.1 copy-start
  231.1 2.7 copy-start.7
  235.2 1.8 copy-start.8
  268.1 99.3 %all-to-all-start.1 = ((bf16[16,2,128,800]{2,3,1,0:T(8,128)(2,1)}), bf16[16,2,128,800]{2,3,1,0:T(8,128)(2,1)}, u32[]{:S(2)}, u32[]{:S(2)}) async-start(bf16[16,2,128,800]{2,3,1,0:T(8,128)(2,1)} %bitcast.86), calls=%async_computation.1 | async-start | bytes 13107200 | tf_op jit(solution)/shard_map/all_to_all | solution.py:152
  272.7 318.0 %all-reduce.8.cloned.1.call-start = ((), (), s32[]{:S(2)}) async-start(), calls=%async_computation.5 | async-start | bytes 6553600 | tf_op jit(solution)/shard_map/psum | solution.py:167
  283.7 1.1 copy-start.4
  283.7 423.5 %all-reduce.6.cloned.1.call-start = ((), (), s32[]{:S(2)}) async-start(), calls=%async_computation.4 | async-start | bytes 3276800 | tf_op jit(solution)/shard_map/psum | solution.py:38
  403.8 11.1 %copy-start.13 = (f32[512]{0:T(512)S(1)}, f32[512]{0:T(512)}, u32[]{:S(2)}) copy-start(f32[512]{0:T(512)} %param.17) | copy-start | bytes 6148
  715.5 3.1 copy-start.14
  715.5 3.7 copy-start.5
Sparse Core Ops, SparseCore 0:
  10.4 101.0 all-gather.1
  114.9 98.2 all-reduce.3
  283.9 306.8 all-reduce.7
  592.9 114.2 all-reduce.5
where the time goes:
time: 731 us; the launch traced here: 729 us
  waiting for transfers between devices  509 us (70%)
  local copies, waits for them, and re-layouts  111 us (15%)
  other arithmetic  52.5 us (7%)
  matrix products  29.1 us (4%)
  between operations  14.8 us (2%)
  starting transfers between devices  12.4 us (2%)
    psum x1, waiting for transfers between devices, per_device(): neg_all = lax.psum(neg_part, ('head', 'tail'))  172 us
    psum x1, waiting for transfers between devices, head_sum(): return lax.psum(tail_grad, 'head')  117 us
    psum x1, waiting for transfers between devices, per_device(): lax.psum(own_negs.astype(jnp.float32).astype(jnp.bfloat16), 'tail')  81.5 us
    all_to_all x1, waiting for transfers between devices, per_device(): lax.all_to_all(outgoing, 'tail', split_axis=0, concat_axis=0, tiled=True)  75.6 us
    all_gather x1, waiting for transfers between devices, per_device(): partition = lax.all_gather(tail_emb, 'tail', axis=0, tiled=True)  62.8 us
  transfers between devices with their start and end apart: 6, of which 5 were waited for; matrix products, arithmetic and copies ran while one was open for 23% of the time, Pallas kernels for 0%

commit v1 on v0

v1 whole, which is shorter than its diff:
```python
import jax
import jax.numpy as jnp
from jax import lax
from jax.sharding import PartitionSpec as P

LEARN_RATE = 0.3


def complex_product(left, right):
    half_width = left.shape[-1] // 2
    left_re, left_im = (left[..., :half_width], left[..., half_width:])
    right_re, right_im = (right[..., :half_width], right[..., half_width:])
    return jnp.concatenate(
        [left_re * right_re - left_im * right_im, left_re * right_im + left_im * right_re], axis=-1
    )


def conj_product(left, right):
    half_width = left.shape[-1] // 2
    left_re, left_im = (left[..., :half_width], left[..., half_width:])
    right_re, right_im = (right[..., :half_width], right[..., half_width:])
    return jnp.concatenate(
        [left_re * right_re + left_im * right_im, left_im * right_re - left_re * right_im], axis=-1
    )


def row_adagrad(embedding, adagrad_state, gradient):
    state_next = adagrad_state + jnp.mean(gradient * gradient, axis=-1)
    updated = (
        embedding.astype(jnp.float32) - LEARN_RATE * gradient / jnp.sqrt(state_next)[..., None]
    )
    return (updated.astype(jnp.bfloat16), state_next)


def per_device(
    head_emb,
    head_state,
    tail_emb,
    tail_state,
    relation_emb,
    head_rows,
    relations,
    tail_offsets,
    tail_owner,
    tail_local,
    block_count,
    neg_blocks,
):
    block_total = tail_local.shape[0]
    edge_count = head_rows.shape[1]
    row_width = head_emb.shape[1]
    span_rows = tail_emb.shape[1]
    owned_blocks = tail_emb.shape[0]
    neg_count = neg_blocks.shape[0]
    peer_count = lax.axis_size("tail")
    head_count = lax.axis_size("head")
    tail_rank = lax.axis_index("tail")
    head_rank = lax.axis_index("head")
    piece = span_rows // head_count
    capacity = max(2, (2 * block_total + peer_count - 1) // peer_count)
    owner_rank = tail_owner[:, 0]
    positions = jnp.arange(block_total, dtype=jnp.int32)
    same_owner = owner_rank[:, None] == owner_rank[None, :]
    earlier = positions[None, :] < positions[:, None]
    slot_index = jnp.sum((same_owner & earlier).astype(jnp.int32), axis=1)
    slot_place = owner_rank * capacity + slot_index
    global_block = owner_rank * owned_blocks + tail_local
    slot_ids = (
        jnp.zeros((peer_count * capacity,), jnp.int32)
        .at[slot_place]
        .set(tail_local)
        .reshape(peer_count, capacity)
    )
    incoming_ids = lax.all_to_all(slot_ids, "tail", split_axis=0, concat_axis=0, tiled=True)

    my_rows = lax.dynamic_slice_in_dim(tail_emb, head_rank * piece, piece, axis=1)
    table = lax.all_gather(
        my_rows.reshape(owned_blocks * piece, row_width), ("head", "tail"), axis=0, tiled=True
    )

    def table_row(block, offset):
        return (
            (offset // piece * peer_count + block // owned_blocks) * owned_blocks
            + block % owned_blocks
        ) * piece + offset % piece

    neg_offset = (
        jnp.arange(head_count, dtype=jnp.int32)[:, None, None] * piece
        + jnp.arange(piece, dtype=jnp.int32)[None, None, :]
    )
    neg_index = table_row(neg_blocks[None, :, None], neg_offset).reshape(-1)
    mine_ids = neg_blocks - tail_rank * owned_blocks

    total_edges = block_total * edge_count
    flat_rows = head_rows.reshape(-1)
    block_of = jnp.arange(total_edges, dtype=jnp.int32) // edge_count
    live_rows = (block_of < block_count[0]).astype(jnp.float32)
    tail_index = block_of * span_rows + tail_offsets.reshape(-1)
    vector_index = table_row(global_block[:, None], tail_offsets).reshape(-1)
    relation_vectors = jnp.take(relation_emb, relations.reshape(-1), axis=0)
    head_vectors = jnp.take(head_emb, flat_rows, axis=0)
    query = complex_product(
        head_vectors.astype(jnp.float32), relation_vectors.astype(jnp.float32)
    ).astype(jnp.bfloat16)

    negatives = jnp.take(table, neg_index, axis=0)
    tail_rows = jnp.take(table, vector_index, axis=0)
    query_float = query.astype(jnp.float32)
    positive = jnp.sum(query_float * tail_rows.astype(jnp.float32), axis=1)
    negative = lax.dot_general(
        query, negatives, (((1,), (1,)), ((), ())), preferred_element_type=jnp.float32
    )
    largest = jnp.maximum(positive, jnp.max(negative, axis=1))
    pos_exp = jnp.exp(positive - largest)
    neg_exp = jnp.exp(negative - largest[:, None])
    denominator = pos_exp + jnp.sum(neg_exp, axis=1)
    pos_grad = (pos_exp / denominator - 1.0) * live_rows
    neg_grad = (neg_exp / denominator[:, None] * live_rows[:, None]).astype(jnp.bfloat16)
    tail_part = pos_grad[:, None] * query_float
    block_grad = (
        jnp.zeros((block_total * span_rows, row_width), jnp.float32)
        .at[tail_index]
        .add(tail_part)
        .astype(jnp.bfloat16)
    )
    outgoing = (
        jnp.zeros((peer_count * capacity, span_rows, row_width), jnp.bfloat16)
        .at[slot_place]
        .set(block_grad.reshape(block_total, span_rows, row_width))
    )
    incoming = lax.all_to_all(
        outgoing.reshape(peer_count, capacity, span_rows, row_width),
        "tail",
        split_axis=0,
        concat_axis=0,
        tiled=True,
    )
    neg_part = lax.dot_general(
        neg_grad, query, (((0,), (0,)), ((), ())), preferred_element_type=jnp.float32
    )
    neg_piece = lax.psum_scatter(neg_part, "head", scatter_dimension=0, tiled=True)
    neg_all = lax.psum(neg_piece, "tail").reshape(neg_count, piece, row_width)

    query_grad = pos_grad[:, None] * tail_rows.astype(jnp.float32) + jnp.dot(
        neg_grad, negatives, preferred_element_type=jnp.float32
    )
    head_grad = (
        jnp.zeros(head_emb.shape, jnp.float32)
        .at[flat_rows]
        .add(conj_product(query_grad, relation_vectors.astype(jnp.float32)))
    )
    head_updated, head_state_updated = row_adagrad(head_emb, head_state, head_grad)
    incoming, head_updated = lax.optimization_barrier((incoming, head_updated))

    arrived = incoming.reshape(peer_count * capacity, head_count, piece, row_width)
    arrived_ids = incoming_ids.reshape(-1)
    tail_grad = jnp.stack(
        [
            jnp.sum(
                jnp.where((arrived_ids == b)[:, None, None, None], arrived.astype(jnp.float32), 0.0),
                axis=0,
            )
            for b in range(owned_blocks)
        ],
        axis=1,
    )
    tail_piece = lax.psum_scatter(
        tail_grad.reshape(head_count * owned_blocks * piece, row_width),
        "head",
        scatter_dimension=0,
        tiled=True,
    ).reshape(owned_blocks, piece, row_width)
    own_negs = jnp.stack(
        [
            jnp.sum(jnp.where((mine_ids == b)[:, None, None], neg_all, 0.0), axis=0)
            for b in range(owned_blocks)
        ],
        axis=0,
    )
    state_rows = lax.dynamic_slice_in_dim(tail_state, head_rank * piece, piece, axis=1)
    tail_updated, tail_state_updated = row_adagrad(my_rows, state_rows, tail_piece + own_negs)
    tail_updated = lax.all_gather(
        tail_updated.reshape(owned_blocks * piece, row_width), "head", axis=0, tiled=True
    )
    tail_updated = (
        tail_updated.reshape(head_count, owned_blocks, piece, row_width)
        .transpose(1, 0, 2, 3)
        .reshape(owned_blocks, span_rows, row_width)
    )
    tail_state_updated = (
        lax.all_gather(tail_state_updated, "head", axis=0, tiled=False)
        .transpose(1, 0, 2)
        .reshape(owned_blocks, span_rows)
    )
    return (head_updated, head_state_updated, tail_updated, tail_state_updated)


def solution(mesh):
    placed = (
        P(("head", "tail"), None),
        P(("head", "tail")),
        P("tail", None, None),
        P("tail", None),
        P(),
        P(("head", "tail"), None),
        P(("head", "tail"), None),
        P(("head", "tail"), None),
        P(("head", "tail"), None),
        P(("head", "tail")),
        P(("head", "tail")),
        P(),
    )
    return jax.shard_map(
        per_device,
        mesh=mesh,
        in_specs=placed,
        out_specs=(
            P(("head", "tail"), None),
            P(("head", "tail")),
            P("tail", None, None),
            P("tail", None),
        ),
        check_vma=False,
    )
```

time: 731 us -> 510 us (0.70)
  waiting for transfers between devices: 509 us -> 304 us
  blocking collectives: 0 us -> 36.4 us
  local copies, waits for them, and re-layouts: 111 us -> 81.4 us
  matrix products: 29.1 us -> 12.6 us
    psum x3 -> x1, waiting for transfers between devices: 370 us -> 78 us  [per_device(): neg_all = lax.psum(neg_piece, 'tail').reshape(neg_count, piece, row_width)]
    reduce_scatter x0 -> x2, waiting for transfers between devices: none -> 58.7 us  [the longest x1 58.7 us: per_device(): lax.psum_scatter(tail_grad.reshape(head_count * owned_blocks * piece, row...]
    all_gather x0 -> x2, blocking collectives: none -> 36.4 us  [the longest x1 18.8 us: per_device(): lax.all_gather(tail_updated.reshape(owned_blocks * piece, row_width), 'he...]
    all_gather x1, waiting for transfers between devices: 62.8 us -> 95.8 us  [per_device(): lax.all_gather(my_rows.reshape(owned_blocks * piece, row_width), ('head',...]
    reshape x3 -> x1, local copies, waits for them, and re-layouts: 24.1 us -> 0.67 us  [per_device(): tail_state_updated = lax.all_gather(tail_state_updated, 'head', axis=0, t...]
    gather x4 -> x3, local copies, waits for them, and re-layouts: 12.8 us -> 29.4 us  [the longest x2 16.6 us: per_device(): tail_rows = jnp.take(table, vector_index, axis=0)]
    dot_general x8 -> x3, matrix products: 29.1 us -> 12.6 us  [the longest x1 4.52 us: per_device(): jnp.dot(neg_grad, negatives, preferred_element_type=jnp.float32)]
    while x22 -> x0, local copies, waits for them, and re-layouts: 16.5 us -> none  [the longest x2 9.24 us: per_device(): lax.scan(score_group, neg_start, (grouped(query), grouped(tail_vectors),...]
  transfers between devices with their start and end apart: 6 -> 6, of which waited for: 5 -> 4; matrix products, arithmetic and copies ran while one was open for 23% -> 25% of each run, Pallas kernels for 0% -> 0%
where the time goes in v1:
time: 510 us; the launch traced here: 509 us
  waiting for transfers between devices  304 us (60%)
  local copies, waits for them, and re-layouts  81.4 us (16%)
  other arithmetic  46.3 us (9%)
  blocking collectives  36.4 us (7%)
  between operations  14.9 us (3%)
  starting transfers between devices  13.1 us (3%)
  matrix products  12.6 us (2%)
    all_gather x1, waiting for transfers between devices, per_device(): lax.all_gather(my_rows.reshape(owned_blocks * piece, row_width), ('head',...  95.8 us
    psum x1, waiting for transfers between devices, per_device(): neg_all = lax.psum(neg_piece, 'tail').reshape(neg_count, piece, row_width)  78 us
    all_to_all x1, waiting for transfers between devices, per_device(): lax.all_to_all(outgoing.reshape(peer_count, capacity, span_rows, row_widt...  71.6 us
    reduce_scatter x1, waiting for transfers between devices, per_device(): lax.psum_scatter(tail_grad.reshape(head_count * owned_blocks * piece, row...  58.7 us
    all_gather x1, blocking collectives, per_device(): lax.all_gather(tail_updated.reshape(owned_blocks * piece, row_width), 'he...  18.8 us
    all_gather x1, blocking collectives, per_device(): lax.all_gather(tail_state_updated, 'head', axis=0, tiled=False)  17.6 us
    gather x2, local copies, waits for them, and re-layouts, per_device(): tail_rows = jnp.take(table, vector_index, axis=0)  16.6 us
    unnamed x49, local copies, waits for them, and re-layouts  13.4 us
  transfers between devices with their start and end apart: 6, of which 4 were waited for; matrix products, arithmetic and copies ran while one was open for 25% of the time, Pallas kernels for 0%

profile of v1, /device:TPU:1, one launch (start us, length us, event | category | flops | bytes accessed | tf_op | source)
XLA Modules:
  0.0 508.9 jit_solution(6795767045325392924)
XLA Ops:
  11.0 7.6 %all-to-all-start.1 = ((s32[16,1,2]{2,1,0:T(1,128)}), s32[16,1,2]{2,1,0:T(1,128)S(1)}, u32[]{:S(2)}, u32[]{:S(2)}) async-start(s32[16,1,2]{2,1,0:T(1,128)} %bitcast.10), calls=%async_computation.1 | async-start | bytes 16384 | tf_op jit(solution)/shard_map/all_to_all | solution.py:74
  20.5 4.1 gather_fusion
  24.5 2.5 copy.137
  27.0 3.0 copy.138
  30.0 5.3 %gather_fusion.1 = bf16[1024,800]{1,0:T(8,128)(2,1)} fusion(bf16[1024,800]{1,0:T(8,128)(2,1)S(1)} %copy.138, s32[1024]{0:T(1024)S(1)} %broadcast_clamp_fusion), kind=kCustom, calls=%fused_computation.3 | custom fusion | bytes 3280896 | tf_op jit(solution)/shard_map/jit(_take)/gather | solution.py:100
  35.3 3.9 copy.139
  40.9 1.7 copy-done.2
  43.5 95.8 %all-gather.4.cloned.1.call-done = bf16[8192,800]{1,0:T(8,128)(2,1)} async-done(((bf16[32,800]{1,0:T(8,128)(2,1)}), bf16[8192,800]{1,0:T(8,128)(2,1)}) %all-gather.4.cloned.1.call-update) | async-done | bytes 13107216 | tf_op jit(solution)/shard_map/all_gather | solution.py:77
  139.3 12.8 %gather_fusion.2 = bf16[1024,800]{1,0:T(8,128)(2,1)} fusion(bf16[8192,800]{1,0:T(8,128)(2,1)} %all-gather.4.cloned.1.call-done, s32[1024]{0:T(1024)S(1)} %fusion.40), kind=kCustom, calls=%fused_computation.clone | custom fusion | bytes 3280896 | tf_op jit(solution)/shard_map/jit(_take)/gather | solution.py:107
  152.1 3.8 copy.141
  155.9 2.1 fusion.5
  158.0 12.8 %gather_fusion.3 = bf16[1024,800]{1,0:T(8,128)(2,1)} fusion(bf16[8192,800]{1,0:T(8,128)(2,1)} %all-gather.4.cloned.1.call-done, s32[1024]{0:T(1024)S(1)} %fusion.41), kind=kCustom, calls=%fused_computation.1.clone | custom fusion | bytes 3280896 | tf_op jit(solution)/shard_map/jit(_take)/gather | solution.py:106
  170.8 3.9 fusion.54
  177.5 4.2 fusion.52
  181.7 2.2 convert_multiply_fusion.2
  183.9 4.9 copy.142
  188.8 10.7 %scatter_custom_fusion = f32[512,800]{1,0:T(8,128)S(1)} fusion(s32[1024]{0:T(1024)S(1)} %bitcast.128, f32[1024,800]{1,0:T(8,128)} %copy.142, f32[]{:T(128)} %constant.175.clone.1), kind=kCustom, calls=%fused_computation.40 | custom fusion | flops 819200 | bytes 1638912 | tf_op jit(solution)/shard_map/scatter-add | solution.py:123
  200.5 1.5 copy.143
  202.1 3.5 broadcast_in_dim.115
  205.6 2.8 scatter_fusion
  208.4 5.1 %all-to-all-start = ((bf16[16,2,128,800]{2,3,1,0:T(8,128)(2,1)}), bf16[16,2,128,800]{2,3,1,0:T(8,128)(2,1)}, u32[]{:S(2)}, u32[]{:S(2)}) async-start(bf16[16,2,128,800]{2,3,1,0:T(8,128)(2,1)} %bitcast.93), calls=%async_computation | async-start | bytes 13107200 | tf_op jit(solution)/shard_map/all_to_all | solution.py:131
  214.3 4.5 fusion.6
  219.9 2.0 pad_maximum_fusion
  221.9 4.9 copy.145
  226.8 10.7 %scatter_custom_fusion.2 = f32[512,800]{1,0:T(8,128)S(1)} fusion(s32[1024]{0:T(1024)S(1)} %bitcast.123, f32[1024,800]{1,0:T(8,128)} %copy.145, f32[]{:T(128)} %constant.175.clone.1), kind=kCustom, calls=%fused_computation.38 | custom fusion | flops 819200 | bytes 1638912 | tf_op jit(solution)/shard_map/scatter-add | solution.py:150
  239.6 71.6 %all-to-all-done = bf16[16,2,128,800]{2,3,1,0:T(8,128)(2,1)} async-done(((bf16[16,2,128,800]{2,3,1,0:T(8,128)(2,1)}), bf16[16,2,128,800]{2,3,1,0:T(8,128)(2,1)}, u32[]{:S(2)}, u32[]{:S(2)}) %all-to-all-start) | async-done | bytes 6553632 | tf_op jit(solution)/shard_map/all_to_all | solution.py:131
  311.3 7.9 %fusion = (f32[128,800]{0,1:T(8,128)S(1)}, f32[128,800]{0,1:T(8,128)S(1)}, f32[128,800]{0,1:T(8,128)S(1)}, f32[128,800]{0,1:T(8,128)S(1)}) fusion(bf16[16,2,128,800]{2,3,1,0:T(8,128)(2,1)} %all-to-all-done, pred[16,2]{1,0:T(8,128)(4,1)S(1)} %copy.148, pred[16,2]{1,0:T(8,128)(4,1)S(1)} %copy.151, pred[16,2]{1,0:T(8,128)(4,1)S(1)} %copy.154, ...), kind=kLoop, calls=%fused_computation.12 | loop fusion | flops 29081600 | bytes 8192128 | tf_op jit(solution)/shard_map/reduce_sum | solution.py:159
  320.1 1.5 copy.159
  323.9 78.0 %all-reduce.2.cloned.1.call-done = f32[8,8,800]{2,1,0:T(8,128)} async-done(((f32[8,8,800]{2,1,0:T(8,128)}), f32[8,8,800]{2,1,0:T(8,128)}) %all-reduce.2.cloned.1.call-update) | async-done | bytes 204816 | tf_op jit(solution)/shard_map/psum | solution.py:142
  403.0 58.7 %reduce-scatter.3.cloned.1.call-done = f32[32,800]{1,0:T(8,128)} async-done(((f32[512,800]{1,0:T(8,128)}), f32[32,800]{1,0:T(8,128)}) %reduce-scatter.3.cloned.1.call-update) | async-done | bytes 102416 | tf_op jit(solution)/shard_map/reduce_scatter | solution.py:167
  463.0 17.6 %all-gather.1 = f32[16,4,8]{2,1,0:T(4,128)S(1)} all-gather(f32[1,4,8]{2,1,0:T(4,128)S(1)} %get-tuple-element.49), channel_id=2, replica_groups=mesh['head'=16,'tail'=16] {'head'}, dimensions={0}, use_global_device_ids=true | all-gather | bytes 2176 | tf_op jit(solution)/shard_map/all_gather | solution.py:191
  482.2 18.8 %all_gather.13 = bf16[512,800]{1,0:T(8,128)(2,1)S(1)} all-gather(bf16[32,800]{1,0:T(8,128)(2,1)S(1)} %fusion.18), channel_id=1, replica_groups=mesh['head'=16,'tail'=16] {'head'}, dimensions={0}, use_global_device_ids=true | all-gather | bytes 870400 | tf_op jit(solution)/shard_map/all_gather | solution.py:182
  (115 shorter events, 23.8 us)
Async XLA Ops:
  7.2 1.2 copy-start
  7.2 2.4 copy-start.17
  7.2 2.6 copy-start.16
  7.2 12.1 %copy-start.11 = (s32[4,256]{1,0:T(4,128)S(1)}, s32[4,256]{1,0:T(4,128)}, u32[]{:S(2)}) copy-start(s32[4,256]{1,0:T(4,128)} %param.21) | copy-start | bytes 12292
  7.2 12.2 %copy-start.12 = (s32[4,256]{1,0:T(4,128)S(1)}, s32[4,256]{1,0:T(4,128)}, u32[]{:S(2)}) copy-start(s32[4,256]{1,0:T(4,128)} %param.20) | copy-start | bytes 12292
  7.2 12.3 %copy-start.13 = (s32[4,256]{1,0:T(4,128)S(1)}, s32[4,256]{1,0:T(4,128)}, u32[]{:S(2)}) copy-start(s32[4,256]{1,0:T(4,128)} %param.19) | copy-start | bytes 12292
  7.2 12.3 %copy-start.18 = (s32[8]{0:T(128)S(1)}, s32[8]{0:T(128)}, u32[]{:S(2)}) copy-start(s32[8]{0:T(128)} %param.25) | copy-start | bytes 100
  7.2 12.6 %copy-start.9 = (bf16[512,800]{0,1:T(8,128)(2,1)S(1)}, bf16[512,800]{0,1:T(8,128)(2,1)}, u32[]{:S(2)}) copy-start(bf16[512,800]{0,1:T(8,128)(2,1)} %param.14) | copy-start | bytes 2457604
  7.3 132.1 %all-gather.4.cloned.1.call-start = ((), (), s32[]{:S(2)}) async-start(), calls=%async_computation.4 | async-start | bytes 14737408 | tf_op jit(solution)/shard_map/all_gather | solution.py:77
  11.0 197.4 %all-to-all-start.1 = ((s32[16,1,2]{2,1,0:T(1,128)}), s32[16,1,2]{2,1,0:T(1,128)S(1)}, u32[]{:S(2)}, u32[]{:S(2)}) async-start(s32[16,1,2]{2,1,0:T(1,128)} %bitcast.10), calls=%async_computation.1 | async-start | bytes 16384 | tf_op jit(solution)/shard_map/all_to_all | solution.py:74
  18.6 292.6 %reduce-scatter.5.cloned.1.call-start = ((), (), s32[]{:S(2)}) async-start(), calls=%async_computation.6 | async-start | bytes 3899392 | tf_op jit(solution)/shard_map/reduce_scatter | solution.py:141
  35.3 4.0 copy-start.5
  39.3 1.4 copy-start.6
  40.9 1.7 copy-start.2
  176.2 1.4 copy-start.8
  208.4 5.9 %copy-start.4 = (bf16[1024,800]{0,1:T(8,128)(2,1)S(1)}, bf16[1024,800]{0,1:T(8,128)(2,1)}, u32[]{:S(2)}) copy-start(bf16[1024,800]{0,1:T(8,128)(2,1)} %copy.141) | copy-start | bytes 4915204
  208.4 102.8 %all-to-all-start = ((bf16[16,2,128,800]{2,3,1,0:T(8,128)(2,1)}), bf16[16,2,128,800]{2,3,1,0:T(8,128)(2,1)}, u32[]{:S(2)}, u32[]{:S(2)}) async-start(bf16[16,2,128,800]{2,3,1,0:T(8,128)(2,1)} %bitcast.93), calls=%async_computation | async-start | bytes 13107200 | tf_op jit(solution)/shard_map/all_to_all | solution.py:131
  213.5 188.4 %all-reduce.2.cloned.1.call-start = ((), (), s32[]{:S(2)}) async-start(), calls=%async_computation.7 | async-start | bytes 458752 | tf_op jit(solution)/shard_map/psum | solution.py:142
  214.3 4.5 copy-start.3
  226.8 10.9 %copy-start.15 = (f32[512]{0:T(512)S(1)}, f32[512]{0:T(512)}, u32[]{:S(2)}) copy-start(f32[512]{0:T(512)} %param.15) | copy-start | bytes 6148
  311.2 150.6 %reduce-scatter.3.cloned.1.call-start = ((), (), s32[]{:S(2)}) async-start(), calls=%async_computation.5 | async-start | bytes 1949696 | tf_op jit(solution)/shard_map/reduce_scatter | solution.py:167
  321.6 1.2 copy-start.7
  321.6 141.3 %copy-start.14 = (f32[4,128]{1,0:T(4,128)S(1)}, f32[4,128]{1,0:T(4,128)}, u32[]{:S(2)}) copy-start(f32[4,128]{1,0:T(4,128)} %param.17) | copy-start | bytes 6148
  321.6 159.7 %copy-start.10 = (bf16[4,8,800]{2,1,0:T(8,128)(2,1)S(1)}, bf16[4,8,800]{2,1,0:T(8,128)(2,1)}, u32[]{:S(2)}) copy-start(bf16[4,8,800]{2,1,0:T(8,128)(2,1)} %copy.164) | copy-start | bytes 153604
  482.2 20.1 %copy-start.1 = (bf16[4,128,800]{1,2,0:T(8,128)(2,1)S(1)}, bf16[4,128,800]{1,2,0:T(8,128)(2,1)}, u32[]{:S(2)}) copy-start(bf16[4,128,800]{1,2,0:T(8,128)(2,1)} %param.16) | copy-start | bytes 2457604
Sparse Core Ops, SparseCore 0:
  12.2 127.0 all-gather.3
  181.8 57.1 reduce-scatter.4
  311.3 90.5 all-reduce.1
  404.4 57.3 reduce-scatter.2
